TPU v7x, 32 devices: a whole 2x2x4 slice. The times are simulated.
32 devices in a mesh: regroup: 2 (over y), loop: 4 (over z), replica: 4 (over x, core).
Axes of the slice: x: 2, y: 2, z: 4, core: 2. Of those that a mesh axis runs over, the one named last changes fastest.
Arguments:
- features: bfloat16 [4, 4, 1024, 256], P('replica', 'loop', None, 'regroup'), may hold values from -6 to 6
- weight: bfloat16 [256, 256], replicated, may hold values from -0.375 to 0.375
- tiles: bfloat16 [4, 4, 2, 32, 128, 128], P('replica', 'loop', 'regroup'), may hold values from 0 to 1, as said below
- tile_row: int32 [4, 4, 2, 32], P('replica', 'loop', 'regroup'), may hold values from 0 to 3, as said below
- tile_col: int32 [4, 4, 2, 32], P('replica', 'loop', 'regroup'), may hold values from 0 to 3, as said below
- tile_width: int32 [4, 4, 2, 32], P('replica', 'loop', 'regroup'), may hold values from 0 to 128, as said below
- cotangent: bfloat16 [4, 4, 2, 512, 256], P('replica', 'loop', 'regroup'), may hold values from -6 to 6
Outputs:
- output: bfloat16 [4, 4, 2, 512, 256], P('replica', 'loop', 'regroup')
- grad_feat: bfloat16 [4, 4, 1024, 256], P('replica', 'loop', None, 'regroup')
- grad_weight: float32 [256, 256], replicated
Inputs may be any that keep to these rules, and one draw needn't show every extreme that they name: `tiles`: entries are 0 or between 0.25 and 1. `tile_row`: slot k < 4 of every device names cell block k. tile_col[r, l, g, s] is l - 1, l or l + 1 modulo 4. `tile_width`: each device's live slots come first, from 4 to 32 of them; some device has exactly 4 live and some all 32; slot 0 is live with width 128.
All inputs are finite; a program needn't handle non-finite values.
Results may differ from a plain program's by a relative error of at most 0.013.
Values may be sent and summed in bfloat16 or wider, within the bound.
A program may use at most 64 MiB of HBM per device.

v0:
```python
import math
import jax
import jax.numpy as jnp
from jax import lax
from jax.sharding import PartitionSpec as P

EPSILON = 1e-06


def shifted(block, axis, distance):
    devices = range(lax.axis_size(axis))
    route = [((i - distance) % len(devices), i) for i in devices]
    return lax.ppermute(block, axis, route)


def rms_scale(values):
    return values * lax.rsqrt(jnp.mean(values * values, axis=-1, keepdims=True) + EPSILON)


def per_device(features, weight, tiles, tile_row, tile_col, tile_width, cotangent):
    cell_rows = lax.all_to_all(features, "regroup", split_axis=2, concat_axis=3, tiled=True)[0, 0]
    cells, width = cell_rows.shape
    edge = tiles.shape[-1]
    blocks = cells // edge
    loops = lax.axis_size("loop")
    high = lax.Precision.HIGHEST
    rows_idx = tile_row[0, 0, 0]
    cols_idx = tile_col[0, 0, 0]
    widths = tile_width[0, 0, 0]
    column = jnp.arange(edge, dtype=jnp.int32)
    live_tiles = jnp.where(
        column[None, None, :] < widths[:, None, None], tiles[0, 0, 0], jnp.zeros((), tiles.dtype)
    )
    row_hot = (rows_idx[:, None] == jnp.arange(blocks, dtype=jnp.int32)[None, :]).astype(
        jnp.float32
    )
    row_sums = jnp.sum(live_tiles, axis=2, dtype=jnp.float32)
    cell_deg = 1.0 + jnp.einsum("tr,ti->ri", row_hot, row_sums, precision=high).reshape(cells)
    cell_root = jnp.sqrt(cell_deg)[:, None]
    col_tile_sums = jnp.sum(live_tiles, axis=1, dtype=jnp.float32)

    def to_nets(values, hot):
        gathered = values.reshape(blocks, edge, width)[rows_idx]
        per_tile = jnp.einsum(
            "tij,tif->tjf", live_tiles, gathered, preferred_element_type=jnp.float32
        )
        return jnp.einsum("tc,tjf->cjf", hot, per_tile, precision=high)

    def from_nets(blocked, index):
        gathered = blocked[index]
        per_tile = jnp.einsum(
            "tij,tjf->tif", live_tiles, gathered, preferred_element_type=jnp.float32
        )
        return jnp.einsum("tr,tif->rif", row_hot, per_tile, precision=high).reshape(cells, width)

    mixed = jnp.dot(cell_rows, weight, preferred_element_type=jnp.float32).astype(jnp.bfloat16)
    scaled = (mixed.astype(jnp.float32) / cell_root).astype(jnp.bfloat16)
    place = (cols_idx - lax.axis_index("loop") + loops) % loops
    net_index = jnp.where(place == 0, 1, jnp.where(place == 1, 2, 0)).astype(jnp.int32)
    near_hot = (net_index[:, None] == jnp.arange(3, dtype=jnp.int32)[None, :]).astype(jnp.float32)
    near_terms = to_nets(scaled, near_hot).astype(jnp.bfloat16)
    near_degs = jnp.einsum("tc,tj->cj", near_hot, col_tile_sums, precision=high).astype(
        jnp.bfloat16
    )
    below = shifted((near_terms[2], near_degs[2]), "loop", 1)
    above = shifted((near_terms[0], near_degs[0]), "loop", -1)
    totals = (
        near_terms[1].astype(jnp.float32)
        + below[0].astype(jnp.float32)
        + above[0].astype(jnp.float32)
    )
    degrees = (
        near_degs[1].astype(jnp.float32)
        + below[1].astype(jnp.float32)
        + above[1].astype(jnp.float32)
    )
    net_deg = (1.0 + degrees)[:, None]
    own_feat = (totals / net_deg).astype(jnp.bfloat16)
    prev_feat = shifted(own_feat, "loop", 1)
    next_feat = shifted(own_feat, "loop", -1)
    net_feat = jnp.stack([prev_feat, own_feat, next_feat])
    gathered_z = from_nets(net_feat, net_index) / cell_root
    normed, norm_back = jax.vjp(rms_scale, gathered_z)
    before = mixed.astype(jnp.float32) + normed
    output = jax.nn.silu(before).astype(jnp.bfloat16)
    sigmoid_v = jax.nn.sigmoid(before)
    grad_before = (
        cotangent[0, 0, 0].astype(jnp.float32) * sigmoid_v * (1.0 + before * (1.0 - sigmoid_v))
    )
    grad_z = norm_back(grad_before)[0]
    grad_scaled = (grad_z / cell_root).astype(jnp.bfloat16)
    grad_near = to_nets(grad_scaled, near_hot).astype(jnp.bfloat16)
    grad_below = shifted(grad_near[2], "loop", 1)
    grad_above = shifted(grad_near[0], "loop", -1)
    grad_sum_own = (
        grad_near[1].astype(jnp.float32)
        + grad_below.astype(jnp.float32)
        + grad_above.astype(jnp.float32)
    )
    grad_own = (grad_sum_own / net_deg).astype(jnp.bfloat16)
    grad_prev = shifted(grad_own, "loop", 1)
    grad_next = shifted(grad_own, "loop", -1)
    grad_net = jnp.stack([grad_prev, grad_own, grad_next])
    grad_mixed = (grad_before + from_nets(grad_net, net_index) / cell_root).astype(jnp.bfloat16)
    grad_rows = jnp.einsum(
        "cg,fg->cf", grad_mixed, weight, preferred_element_type=jnp.float32
    ).astype(jnp.bfloat16)
    grad_feat = lax.all_to_all(
        grad_rows[None, None], "regroup", split_axis=3, concat_axis=2, tiled=True
    )
    weight_term = jnp.einsum("cf,cg->fg", cell_rows, grad_mixed, preferred_element_type=jnp.float32)
    weight_part = lax.psum_scatter(
        weight_term, ("regroup", "loop"), scatter_dimension=0, tiled=True
    )
    weight_part = lax.psum(weight_part, "replica")
    weight_sum = lax.all_gather(weight_part, ("regroup", "loop"), axis=0, tiled=True)
    total_cells = cells * lax.axis_size("regroup") * loops * lax.axis_size("replica")
    grad_weight = weight_sum * (1.0 / math.sqrt(total_cells))
    return (output[None, None, None], grad_feat, grad_weight)


def solution(mesh):
    return jax.shard_map(
        per_device,
        mesh=mesh,
        in_specs=(
            P("replica", "loop", None, "regroup"),
            P(),
            P("replica", "loop", "regroup", None, None, None),
            P("replica", "loop", "regroup", None),
            P("replica", "loop", "regroup", None),
            P("replica", "loop", "regroup", None),
            P("replica", "loop", "regroup", None, None),
        ),
        out_specs=(
            P("replica", "loop", "regroup", None, None),
            P("replica", "loop", None, "regroup"),
            P(),
        ),
        check_vma=False,
    )
```

profile of v0, /device:TPU:0, one launch (start us, length us, event | category | flops | bytes accessed | tf_op | source)
XLA Modules:
  0.0 198.6 jit_solution(6420533877653232573)
XLA Ops:
  8.6 1.6 convert_reduce_fusion
  11.0 3.0 %collective-permute-start.2 = (bf16[128]{0:T(256)(128)(2,1)}, bf16[128]{0:T(256)(128)(2,1)}, u32[]{:S(2)}, u32[]{:S(2)}) collective-permute-start(bf16[128]{0:T(256)(128)(2,1)} %get-tuple-element.22), channel_id=1, source_target_pairs={{12,0},{0,4},{4,8},{8,12},{13,1},{1,5},{5,9},{9,13},{14,2},{2,6},{... | collective-permute-start | bytes 776 | tf_op jit(solution)/shard_map/ppermute | solution.py:13
  14.0 2.0 %collective-permute-start.3 = (bf16[128]{0:T(256)(128)(2,1)}, bf16[128]{0:T(256)(128)(2,1)}, u32[]{:S(2)}, u32[]{:S(2)}) collective-permute-start(bf16[128]{0:T(256)(128)(2,1)} %get-tuple-element.23), channel_id=1, source_target_pairs={{4,0},{8,4},{12,8},{0,12},{5,1},{9,5},{13,9},{1,13},{6,2},{10,6},{... | collective-permute-start | bytes 776 | tf_op jit(solution)/shard_map/ppermute | solution.py:13
  16.0 1.4 copy.130
  17.9 2.3 %reduce.1 = bf16[1024,128]{1,0:T(8,128)(2,1)S(1)} reduce(bf16[1024,1,1,128]{3,2,1,0:T(2,128)(2,1)S(1)} %bitcast.136, bf16[]{:T(256)} %broadcast.232), dimensions={1,2}, to_apply=%bitcast.131.reduce_sub_computation | reduce | bytes 524290
  20.9 3.4 %all-to-all-start = ((bf16[2,2,32768]{2,1,0:T(2,128)(2,1)}), bf16[2,2,32768]{2,1,0:T(2,128)(2,1)S(1)}, u32[]{:S(2)}, u32[]{:S(2)}) async-start(bf16[2,2,32768]{2,1,0:T(2,128)(2,1)} %reshape.232), calls=%async_computation | async-start | bytes 524288 | tf_op jit(solution)/shard_map/all_to_all | solution.py:21
  25.9 3.6 %all-to-all-done = bf16[2,2,32768]{2,1,0:T(2,128)(2,1)S(1)} async-done(((bf16[2,2,32768]{2,1,0:T(2,128)(2,1)}), bf16[2,2,32768]{2,1,0:T(2,128)(2,1)S(1)}, u32[]{:S(2)}, u32[]{:S(2)}) %all-to-all-start) | async-done | bytes 262176 | tf_op jit(solution)/shard_map/all_to_all | solution.py:21
  30.0 1.1 divide_convert_fusion
  33.1 3.8 %fusion.9 = bf16[3,128,256]{2,0,1:T(4,128)(2,1)S(1)} fusion(f32[32,128,256]{2,1,0:T(8,128)S(1)} %fusion.23, s32[32]{0:T(128)S(1)} %copy-done.10), kind=kOutput, calls=%fused_computation.17 | convolution fusion | flops 37847136 | bytes 4391040 | tf_op jit(solution)/shard_map/tc,tjf->cjf/dot_general | solution.py:47
  37.3 2.1 %collective-permute-start.1 = (bf16[128,256]{1,0:T(8,128)(2,1)S(1)}, bf16[128,256]{1,0:T(8,128)(2,1)S(1)}, u32[]{:S(2)}, u32[]{:S(2)}) collective-permute-start(bf16[128,256]{1,0:T(8,128)(2,1)S(1)} %bitcast.146), channel_id=1, source_target_pairs={{4,0},{8,4},{12,8},{0,12},{5,1},{9,5},{13,9},{1,13},{6,2},{10,6},{... | collective-permute-start | bytes 196616 | tf_op jit(solution)/shard_map/ppermute | solution.py:13
  40.0 1.6 collective-permute-done.1
  41.6 3.8 %collective-permute-done = bf16[128,256]{1,0:T(8,128)(2,1)S(1)} collective-permute-done((bf16[128,256]{1,0:T(8,128)(2,1)S(1)}, bf16[128,256]{1,0:T(8,128)(2,1)S(1)}, u32[]{:S(2)}, u32[]{:S(2)}) %collective-permute-start) | collective-permute-done | bytes 65568 | tf_op jit(solution)/shard_map/ppermute | solution.py:13
  45.6 2.0 %collective-permute-start.4 = (bf16[128,256]{1,0:T(8,128)(2,1)S(1)}, bf16[128,256]{1,0:T(8,128)(2,1)S(1)}, u32[]{:S(2)}, u32[]{:S(2)}) collective-permute-start(bf16[128,256]{1,0:T(8,128)(2,1)S(1)} %fusion.27), channel_id=1, source_target_pairs={{12,0},{0,4},{4,8},{8,12},{13,1},{1,5},{5,9},{9,13},{14,2},{2,6},{... | collective-permute-start | bytes 196616 | tf_op jit(solution)/shard_map/ppermute | solution.py:13
  47.6 2.2 %collective-permute-done.5 = bf16[128,256]{1,0:T(8,128)(2,1)S(1)} collective-permute-done((bf16[128,256]{1,0:T(8,128)(2,1)S(1)}, bf16[128,256]{1,0:T(8,128)(2,1)S(1)}, u32[]{:S(2)}, u32[]{:S(2)}) %collective-permute-start.5) | collective-permute-done | bytes 65568 | tf_op jit(solution)/shard_map/ppermute | solution.py:13
  49.8 2.0 %collective-permute-done.4 = bf16[128,256]{1,0:T(8,128)(2,1)S(1)} collective-permute-done((bf16[128,256]{1,0:T(8,128)(2,1)S(1)}, bf16[128,256]{1,0:T(8,128)(2,1)S(1)}, u32[]{:S(2)}, u32[]{:S(2)}) %collective-permute-start.4) | collective-permute-done | bytes 65568 | tf_op jit(solution)/shard_map/ppermute | solution.py:13
  53.5 4.0 %fusion.19 = (f32[4,128]{0,1:T(8,128)S(1)}, f32[4,128,256]{2,0,1:T(4,128)S(1)}) fusion(f32[4,128]{0,1:T(8,128)S(1)} %copy-done.8, f32[32,128,256]{2,1,0:T(8,128)S(1)} %fusion.22, s32[32]{0:T(128)S(1)} %bitcast.156), kind=kOutput, calls=%fused_computation.39 | convolution fusion | flops 50724480 | bytes 4722816 | tf_op jit(solution)/shard_map/tr,tif->rif/dot_general | solution.py:54
  57.7 1.1 multiply_reduce_fusion
  61.1 3.8 %fusion.2 = bf16[3,128,256]{2,0,1:T(4,128)(2,1)S(1)} fusion(f32[32,128,256]{2,1,0:T(8,128)S(1)} %fusion.21, s32[32]{0:T(128)S(1)} %copy-done.11), kind=kOutput, calls=%fused_computation.6 | convolution fusion | flops 37748832 | bytes 4391040 | tf_op jit(solution)/shard_map/tc,tjf->cjf/dot_general | solution.py:47
  65.0 3.8 %collective-permute-start.7 = (bf16[128,256]{1,0:T(8,128)(2,1)S(1)}, bf16[128,256]{1,0:T(8,128)(2,1)S(1)}, u32[]{:S(2)}, u32[]{:S(2)}) collective-permute-start(bf16[128,256]{1,0:T(8,128)(2,1)S(1)} %get-tuple-element.21), channel_id=1, source_target_pairs={{4,0},{8,4},{12,8},{0,12},{5,1},{9,5},{13,9},{1,13},{6,2},{10,6},{... | collective-permute-start | bytes 196616 | tf_op jit(solution)/shard_map/ppermute | solution.py:13
  68.9 2.2 %collective-permute-done.6 = bf16[128,256]{1,0:T(8,128)(2,1)S(1)} collective-permute-done((bf16[128,256]{1,0:T(8,128)(2,1)S(1)}, bf16[128,256]{1,0:T(8,128)(2,1)S(1)}, u32[]{:S(2)}, u32[]{:S(2)}) %collective-permute-start.6) | collective-permute-done | bytes 65568 | tf_op jit(solution)/shard_map/ppermute | solution.py:13
  71.2 4.2 %collective-permute-start.9 = (bf16[128,256]{1,0:T(8,128)(2,1)S(1)}, bf16[128,256]{1,0:T(8,128)(2,1)S(1)}, u32[]{:S(2)}, u32[]{:S(2)}) collective-permute-start(bf16[128,256]{1,0:T(8,128)(2,1)S(1)} %fusion.30), channel_id=1, source_target_pairs={{4,0},{8,4},{12,8},{0,12},{5,1},{9,5},{13,9},{1,13},{6,2},{10,6},{... | collective-permute-start | bytes 196616 | tf_op jit(solution)/shard_map/ppermute | solution.py:13
  75.4 1.9 collective-permute-done.9
  77.3 4.2 %collective-permute-done.8 = bf16[128,256]{1,0:T(8,128)(2,1)S(1)} collective-permute-done((bf16[128,256]{1,0:T(8,128)(2,1)S(1)}, bf16[128,256]{1,0:T(8,128)(2,1)S(1)}, u32[]{:S(2)}, u32[]{:S(2)}) %collective-permute-start.8) | collective-permute-done | bytes 65568 | tf_op jit(solution)/shard_map/ppermute | solution.py:13
  82.9 3.8 %fusion = f32[4,128,256]{2,0,1:T(4,128)S(1)} fusion(f32[32,128,256]{2,1,0:T(8,128)S(1)} %fusion.20, s32[32]{0:T(128)S(1)} %bitcast.157), kind=kOutput, calls=%fused_computation.4 | convolution fusion | flops 50331776 | bytes 4718720 | tf_op jit(solution)/shard_map/tr,tif->rif/dot_general | solution.py:54
  87.9 0.8 copy.102
  89.5 2.2 %reduce.2 = bf16[256,512]{1,0:T(8,128)(2,1)S(1)} reduce(bf16[256,1,1,512]{3,2,1,0:T(2,128)(2,1)S(1)} %bitcast.137, bf16[]{:T(256)} %broadcast.232), dimensions={1,2}, to_apply=%bitcast.110.reduce_sub_computation | reduce | bytes 524290
  91.9 7.6 %all_to_all.33 = bf16[2,2,32768]{2,1,0:T(2,128)(2,1)S(1)} all-to-all(bf16[2,2,32768]{2,1,0:T(2,128)(2,1)S(1)} %reshape.234), channel_id=1, replica_groups=mesh['regroup'=2,'loop'=4,'replica'=4] {'regroup'}, dimensions={0} | all-to-all | bytes 524288 | tf_op jit(solution)/shard_map/all_to_all | solution.py:108
  99.8 0.8 copy.98
  100.6 46.8 %reduce-scatter.4.cloned.1.call-done = f32[32,256]{1,0:T(8,128)} async-done(((f32[256,256]{1,0:T(8,128)}), f32[32,256]{1,0:T(8,128)}) %reduce-scatter.4.cloned.1.call-update) | async-done | bytes 32784
  147.4 0.9 copy.103
  148.2 11.5 %psum.7 = f32[32,256]{0,1:T(8,128)S(1)} all-reduce(f32[32,256]{0,1:T(8,128)S(1)} %copy.103), channel_id=1, replica_groups=mesh['regroup'=2,'loop'=4,'replica'=4] {'replica'}, use_global_device_ids=true, to_apply=%region_5.6 | all-reduce | flops 8192 | bytes 65536 | tf_op jit(solution)/shard_map/psum | solution.py:115
  159.8 31.3 %all_gather.3 = f32[256,256]{1,0:T(8,128)S(1)} all-gather(f32[32,256]{1,0:T(8,128)S(1)} %copy.99), channel_id=1, replica_groups=mesh['regroup'=2,'loop'=4,'replica'=4] {'regroup','loop'}, dimensions={0}, use_global_device_ids=true | all-gather | bytes 294912 | tf_op jit(solution)/shard_map/all_gather | solution.py:116
  (96 shorter events, 17.3 us)
Async XLA Ops:
  7.2 22.9 %copy-start = (bf16[256,256]{1,0:T(8,128)(2,1)S(1)}, bf16[256,256]{1,0:T(8,128)(2,1)}, u32[]{:S(2)}) copy-start(bf16[256,256]{1,0:T(8,128)(2,1)} %param.8) | copy-start | bytes 393220
  7.2 17.3 %copy-start.18 = (s32[1,1,1,32]{3,2,1,0:T(1,128)S(1)}, s32[1,1,1,32]{3,2,1,0:T(1,128)}, u32[]{:S(2)}) copy-start(s32[1,1,1,32]{3,2,1,0:T(1,128)} %param.11) | copy-start | bytes 388
  7.2 17.8 %copy-start.14 = (s32[1,1,1,32]{3,2,1,0:T(1,128)S(1)}, s32[1,1,1,32]{3,2,1,0:T(1,128)}, u32[]{:S(2)}) copy-start(s32[1,1,1,32]{3,2,1,0:T(1,128)} %param.10) | copy-start | bytes 388
  8.6 16.4 %copy-start.9 = (s32[32]{0:T(128)}, s32[32]{0:T(128)S(1)}, u32[]{:S(2)}) copy-start(s32[32]{0:T(128)S(1)} %compare_select_fusion.8) | copy-start | bytes 388
  11.0 28.4 %collective-permute-start.2 = (bf16[128]{0:T(256)(128)(2,1)}, bf16[128]{0:T(256)(128)(2,1)}, u32[]{:S(2)}, u32[]{:S(2)}) collective-permute-start(bf16[128]{0:T(256)(128)(2,1)} %get-tuple-element.22), channel_id=1, source_target_pairs={{12,0},{0,4},{4,8},{8,12},{13,1},{1,5},{5,9},{9,13},{14,2},{2,6},{... | collective-permute-start | bytes 776 | tf_op jit(solution)/shard_map/ppermute | solution.py:13
  14.0 25.4 %collective-permute-start.3 = (bf16[128]{0:T(256)(128)(2,1)}, bf16[128]{0:T(256)(128)(2,1)}, u32[]{:S(2)}, u32[]{:S(2)}) collective-permute-start(bf16[128]{0:T(256)(128)(2,1)} %get-tuple-element.23), channel_id=1, source_target_pairs={{4,0},{8,4},{12,8},{0,12},{5,1},{9,5},{13,9},{1,13},{6,2},{10,6},{... | collective-permute-start | bytes 776 | tf_op jit(solution)/shard_map/ppermute | solution.py:13
  20.9 8.6 %all-to-all-start = ((bf16[2,2,32768]{2,1,0:T(2,128)(2,1)}), bf16[2,2,32768]{2,1,0:T(2,128)(2,1)S(1)}, u32[]{:S(2)}, u32[]{:S(2)}) async-start(bf16[2,2,32768]{2,1,0:T(2,128)(2,1)} %reshape.232), calls=%async_computation | async-start | bytes 524288 | tf_op jit(solution)/shard_map/all_to_all | solution.py:21
  24.4 123.0 %reduce-scatter.4.cloned.1.call-start = ((), (), s32[]{:S(2)}) async-start(), calls=%async_computation.3 | async-start | bytes 294912
  30.0 1.1 copy-start.4
  31.1 1.2 copy-start.1
  32.3 0.8 copy-start.10
  33.1 14.5 %copy-start.17 = (s32[32]{0:T(128)S(1)}, s32[32]{0:T(128)}, u32[]{:S(2)}) copy-start(s32[32]{0:T(128)} %fusion.43) | copy-start | bytes 388
  37.3 4.3 %collective-permute-start.1 = (bf16[128,256]{1,0:T(8,128)(2,1)S(1)}, bf16[128,256]{1,0:T(8,128)(2,1)S(1)}, u32[]{:S(2)}, u32[]{:S(2)}) collective-permute-start(bf16[128,256]{1,0:T(8,128)(2,1)S(1)} %bitcast.146), channel_id=1, source_target_pairs={{4,0},{8,4},{12,8},{0,12},{5,1},{9,5},{13,9},{1,13},{6,2},{10,6},{... | collective-permute-start | bytes 196616 | tf_op jit(solution)/shard_map/ppermute | solution.py:13
  39.4 6.1 %collective-permute-start = (bf16[128,256]{1,0:T(8,128)(2,1)S(1)}, bf16[128,256]{1,0:T(8,128)(2,1)S(1)}, u32[]{:S(2)}, u32[]{:S(2)}) collective-permute-start(bf16[128,256]{1,0:T(8,128)(2,1)S(1)} %bitcast.145), channel_id=1, source_target_pairs={{12,0},{0,4},{4,8},{8,12},{13,1},{1,5},{5,9},{9,13},{14,2},{2,6},{... | collective-permute-start | bytes 196616 | tf_op jit(solution)/shard_map/ppermute | solution.py:13
  40.0 11.9 %copy-start.12 = (f32[128]{0:T(128)}, f32[128]{0:T(128)S(1)}, u32[]{:S(2)}) copy-start(f32[128]{0:T(128)S(1)} %fusion.48) | copy-start | bytes 1540
  45.5 4.3 %collective-permute-start.5 = (bf16[128,256]{1,0:T(8,128)(2,1)S(1)}, bf16[128,256]{1,0:T(8,128)(2,1)S(1)}, u32[]{:S(2)}, u32[]{:S(2)}) collective-permute-start(bf16[128,256]{1,0:T(8,128)(2,1)S(1)} %fusion.27), channel_id=1, source_target_pairs={{4,0},{8,4},{12,8},{0,12},{5,1},{9,5},{13,9},{1,13},{6,2},{10,6},{... | collective-permute-start | bytes 196616 | tf_op jit(solution)/shard_map/ppermute | solution.py:13
  45.6 6.3 %collective-permute-start.4 = (bf16[128,256]{1,0:T(8,128)(2,1)S(1)}, bf16[128,256]{1,0:T(8,128)(2,1)S(1)}, u32[]{:S(2)}, u32[]{:S(2)}) collective-permute-start(bf16[128,256]{1,0:T(8,128)(2,1)S(1)} %fusion.27), channel_id=1, source_target_pairs={{12,0},{0,4},{4,8},{8,12},{13,1},{1,5},{5,9},{9,13},{14,2},{2,6},{... | collective-permute-start | bytes 196616 | tf_op jit(solution)/shard_map/ppermute | solution.py:13
  52.6 0.8 copy-start.8
  52.6 0.8 copy-start.15
  53.4 4.2 %copy-start.6 = (f32[512,256]{1,0:T(8,128)S(1)}, f32[512,256]{1,0:T(8,128)}, u32[]{:S(2)}) copy-start(f32[512,256]{1,0:T(8,128)} %get-tuple-element.25) | copy-start | bytes 1572868
  53.5 4.2 %copy-start.7 = (bf16[1,1,1,512,256]{4,3,2,1,0:T(8,128)(2,1)S(1)}, bf16[1,1,1,512,256]{4,3,2,1,0:T(8,128)(2,1)}, u32[]{:S(2)}) copy-start(bf16[1,1,1,512,256]{4,3,2,1,0:T(8,128)(2,1)} %param.13) | copy-start | bytes 786436
  58.8 0.8 copy-start.2
  60.3 0.8 copy-start.11
  61.1 10.0 %copy-start.13 = (f32[128]{0:T(128)S(1)}, f32[128]{0:T(128)}, u32[]{:S(2)}) copy-start(f32[128]{0:T(128)} %copy-done.12) | copy-start | bytes 1540
  65.0 6.1 %collective-permute-start.6 = (bf16[128,256]{1,0:T(8,128)(2,1)S(1)}, bf16[128,256]{1,0:T(8,128)(2,1)S(1)}, u32[]{:S(2)}, u32[]{:S(2)}) collective-permute-start(bf16[128,256]{1,0:T(8,128)(2,1)S(1)} %get-tuple-element.20), channel_id=1, source_target_pairs={{12,0},{0,4},{4,8},{8,12},{13,1},{1,5},{5,9},{9,13},{14,2},{2,6},{... | collective-permute-start | bytes 196616 | tf_op jit(solution)/shard_map/ppermute | solution.py:13
  65.0 6.1 %collective-permute-start.7 = (bf16[128,256]{1,0:T(8,128)(2,1)S(1)}, bf16[128,256]{1,0:T(8,128)(2,1)S(1)}, u32[]{:S(2)}, u32[]{:S(2)}) collective-permute-start(bf16[128,256]{1,0:T(8,128)(2,1)S(1)} %get-tuple-element.21), channel_id=1, source_target_pairs={{4,0},{8,4},{12,8},{0,12},{5,1},{9,5},{13,9},{1,13},{6,2},{10,6},{... | collective-permute-start | bytes 196616 | tf_op jit(solution)/shard_map/ppermute | solution.py:13
  71.2 6.1 %collective-permute-start.9 = (bf16[128,256]{1,0:T(8,128)(2,1)S(1)}, bf16[128,256]{1,0:T(8,128)(2,1)S(1)}, u32[]{:S(2)}, u32[]{:S(2)}) collective-permute-start(bf16[128,256]{1,0:T(8,128)(2,1)S(1)} %fusion.30), channel_id=1, source_target_pairs={{4,0},{8,4},{12,8},{0,12},{5,1},{9,5},{13,9},{1,13},{6,2},{10,6},{... | collective-permute-start | bytes 196616 | tf_op jit(solution)/shard_map/ppermute | solution.py:13
  75.4 6.1 %collective-permute-start.8 = (bf16[128,256]{1,0:T(8,128)(2,1)S(1)}, bf16[128,256]{1,0:T(8,128)(2,1)S(1)}, u32[]{:S(2)}, u32[]{:S(2)}) collective-permute-start(bf16[128,256]{1,0:T(8,128)(2,1)S(1)} %fusion.30), channel_id=1, source_target_pairs={{12,0},{0,4},{4,8},{8,12},{13,1},{1,5},{5,9},{9,13},{14,2},{2,6},{... | collective-permute-start | bytes 196616 | tf_op jit(solution)/shard_map/ppermute | solution.py:13
  82.1 0.7 copy-start.16
  82.9 3.9 %copy-start.3 = (f32[512,256]{1,0:T(8,128)S(1)}, f32[512,256]{1,0:T(8,128)}, u32[]{:S(2)}) copy-start(f32[512,256]{1,0:T(8,128)} %copy-done.2) | copy-start | bytes 1572868
  86.7 1.0 copy-start.5
Sparse Core Ops, SparseCore 0:
  88.9 58.4 reduce-scatter.3
where the time goes:
time: 199 us
  waiting for transfers between devices  68.4 us (34%)
  blocking collectives  50.3 us (25%)
  starting transfers between devices  20.7 us (10%)
  matrix products  20.2 us (10%)
  between operations  14.5 us (7%)
  local copies, waits for them, and re-layouts  12.9 us (6%)
  other arithmetic  11.6 us (6%)
    unnamed x2, waiting for transfers between devices  46.8 us
    all_gather x1, blocking collectives, per_device(): lax.all_gather(weight_part, ('regroup', 'loop'), axis=0, tiled=True)  31.3 us
    ppermute x10, waiting for transfers between devices, shifted(): return lax.ppermute(block, axis, route)  18 us
    ppermute x10, starting transfers between devices, shifted(): return lax.ppermute(block, axis, route)  17.2 us
    psum x1, blocking collectives, per_device(): weight_part = lax.psum(weight_part, 'replica')  11.5 us
    dot_general x2, matrix products, from_nets(): jnp.einsum('tr,tif->rif', row_hot, per_tile, precision=high)  7.83 us
    dot_general x2, matrix products, to_nets(): return jnp.einsum('tc,tjf->cjf', hot, per_tile, precision=high)  7.66 us
    all_to_all x1, blocking collectives, per_device(): lax.all_to_all(grad_rows[None, None], 'regroup', split_axis=3, concat_axi...  7.56 us
  transfers between devices with their start and end apart: 12, of which 9 were waited for; matrix products, arithmetic and copies ran while one was open for 9% of the time, Pallas kernels for 0%

commit v1 on v0

--- a/solution.py
+++ b/solution.py
@@ -5,6 +5,11 @@
 from jax.sharding import PartitionSpec as P
 
 EPSILON = 1e-06
+
+
+def gather_and_add(x, axis):
+    blocks = lax.all_gather(x, axis)
+    return jnp.sum(blocks, axis=0)
 
 
 def shifted(block, axis, distance):
@@ -112,7 +117,7 @@
     weight_part = lax.psum_scatter(
         weight_term, ("regroup", "loop"), scatter_dimension=0, tiled=True
     )
-    weight_part = lax.psum(weight_part, "replica")
+    weight_part = gather_and_add(weight_part, "replica")
     weight_sum = lax.all_gather(weight_part, ("regroup", "loop"), axis=0, tiled=True)
     total_cells = cells * lax.axis_size("regroup") * loops * lax.axis_size("replica")
     grad_weight = weight_sum * (1.0 / math.sqrt(total_cells))

time: 199 us -> 192 us (0.965)
  blocking collectives: 50.3 us -> 44.5 us
    unnamed x2 -> x1, waiting for transfers between devices: 46.8 us -> 0.02 us
    reduce_scatter x0 -> x1, waiting for transfers between devices: none -> 46.7 us  [per_device(): lax.psum_scatter(weight_term, ('regroup', 'loop'), scatter_dimension=0, t...]
    psum x1 -> x0, blocking collectives: 11.5 us -> none  [per_device(): weight_part = lax.psum(weight_part, 'replica')]
    all_gather x0 -> x1, blocking collectives: none -> 5.62 us  [gather_and_add(): blocks = lax.all_gather(x, axis)]
    unnamed x51 -> x50, local copies, waits for them, and re-layouts: 7.11 us -> 6.26 us
  transfers between devices with their start and end apart: 12 -> 12, of which waited for: 9 -> 9; matrix products, arithmetic and copies ran while one was open for 9% -> 10% of each run, Pallas kernels for 0% -> 0%
where the time goes in v1:
time: 192 us
  waiting for transfers between devices  68.3 us (36%)
  blocking collectives  44.5 us (23%)
  starting transfers between devices  20.7 us (11%)
  matrix products  20.2 us (11%)
  between operations  14.5 us (8%)
  local copies, waits for them, and re-layouts  12 us (6%)
  other arithmetic  11.6 us (6%)
    reduce_scatter x1, waiting for transfers between devices, per_device(): lax.psum_scatter(weight_term, ('regroup', 'loop'), scatter_dimension=0, t...  46.7 us
    all_gather x1, blocking collectives, per_device(): lax.all_gather(weight_part, ('regroup', 'loop'), axis=0, tiled=True)  31.3 us
    ppermute x10, waiting for transfers between devices, shifted(): return lax.ppermute(block, axis, route)  18 us
    ppermute x10, starting transfers between devices, shifted(): return lax.ppermute(block, axis, route)  17.2 us
    dot_general x2, matrix products, from_nets(): jnp.einsum('tr,tif->rif', row_hot, per_tile, precision=high)  7.81 us
    dot_general x2, matrix products, to_nets(): return jnp.einsum('tc,tjf->cjf', hot, per_tile, precision=high)  7.66 us
    all_to_all x1, blocking collectives, per_device(): lax.all_to_all(grad_rows[None, None], 'regroup', split_axis=3, concat_axi...  7.56 us
    unnamed x50, local copies, waits for them, and re-layouts  6.26 us
  transfers between devices with their start and end apart: 12, of which 9 were waited for; matrix products, arithmetic and copies ran while one was open for 10% of the time, Pallas kernels for 0%

profile of v1, /device:TPU:0, one launch (start us, length us, event | category | flops | bytes accessed | tf_op | source)
XLA Modules:
  0.0 191.9 jit_solution(16814617880006446578)
XLA Ops:
  8.6 1.6 convert_reduce_fusion
  11.0 3.0 %collective-permute-start.2 = (bf16[128]{0:T(256)(128)(2,1)}, bf16[128]{0:T(256)(128)(2,1)}, u32[]{:S(2)}, u32[]{:S(2)}) collective-permute-start(bf16[128]{0:T(256)(128)(2,1)} %get-tuple-element.13), channel_id=1, source_target_pairs={{12,0},{0,4},{4,8},{8,12},{13,1},{1,5},{5,9},{9,13},{14,2},{2,6},{... | collective-permute-start | bytes 776 | tf_op jit(solution)/shard_map/ppermute | solution.py:18
  14.0 2.0 %collective-permute-start.3 = (bf16[128]{0:T(256)(128)(2,1)}, bf16[128]{0:T(256)(128)(2,1)}, u32[]{:S(2)}, u32[]{:S(2)}) collective-permute-start(bf16[128]{0:T(256)(128)(2,1)} %get-tuple-element.14), channel_id=1, source_target_pairs={{4,0},{8,4},{12,8},{0,12},{5,1},{9,5},{13,9},{1,13},{6,2},{10,6},{... | collective-permute-start | bytes 776 | tf_op jit(solution)/shard_map/ppermute | solution.py:18
  16.0 1.4 copy.129
  17.9 2.3 %reduce.1 = bf16[1024,128]{1,0:T(8,128)(2,1)S(1)} reduce(bf16[1024,1,1,128]{3,2,1,0:T(2,128)(2,1)S(1)} %bitcast.137, bf16[]{:T(256)} %broadcast.232), dimensions={1,2}, to_apply=%bitcast.132.reduce_sub_computation | reduce | bytes 524290
  20.2 0.8 reshape.233
  20.9 3.4 %all-to-all-start = ((bf16[2,2,32768]{2,1,0:T(2,128)(2,1)}), bf16[2,2,32768]{2,1,0:T(2,128)(2,1)S(1)}, u32[]{:S(2)}, u32[]{:S(2)}) async-start(bf16[2,2,32768]{2,1,0:T(2,128)(2,1)} %reshape.233), calls=%async_computation | async-start | bytes 524288 | tf_op jit(solution)/shard_map/all_to_all | solution.py:26
  25.9 3.6 %all-to-all-done = bf16[2,2,32768]{2,1,0:T(2,128)(2,1)S(1)} async-done(((bf16[2,2,32768]{2,1,0:T(2,128)(2,1)}), bf16[2,2,32768]{2,1,0:T(2,128)(2,1)S(1)}, u32[]{:S(2)}, u32[]{:S(2)}) %all-to-all-start) | async-done | bytes 262176 | tf_op jit(solution)/shard_map/all_to_all | solution.py:26
  30.0 1.1 divide_convert_fusion
  33.1 3.8 %fusion.9 = bf16[3,128,256]{2,0,1:T(4,128)(2,1)S(1)} fusion(f32[32,128,256]{2,1,0:T(8,128)S(1)} %fusion.23, s32[32]{0:T(128)S(1)} %copy-done.10), kind=kOutput, calls=%fused_computation.17 | convolution fusion | flops 37847136 | bytes 4391040 | tf_op jit(solution)/shard_map/tc,tjf->cjf/dot_general | solution.py:52
  37.3 2.1 %collective-permute-start.1 = (bf16[128,256]{1,0:T(8,128)(2,1)S(1)}, bf16[128,256]{1,0:T(8,128)(2,1)S(1)}, u32[]{:S(2)}, u32[]{:S(2)}) collective-permute-start(bf16[128,256]{1,0:T(8,128)(2,1)S(1)} %bitcast.148), channel_id=1, source_target_pairs={{4,0},{8,4},{12,8},{0,12},{5,1},{9,5},{13,9},{1,13},{6,2},{10,6},{... | collective-permute-start | bytes 196616 | tf_op jit(solution)/shard_map/ppermute | solution.py:18
  40.0 1.6 collective-permute-done.1
  41.6 3.8 %collective-permute-done = bf16[128,256]{1,0:T(8,128)(2,1)S(1)} collective-permute-done((bf16[128,256]{1,0:T(8,128)(2,1)S(1)}, bf16[128,256]{1,0:T(8,128)(2,1)S(1)}, u32[]{:S(2)}, u32[]{:S(2)}) %collective-permute-start) | collective-permute-done | bytes 65568 | tf_op jit(solution)/shard_map/ppermute | solution.py:18
  45.6 2.0 %collective-permute-start.4 = (bf16[128,256]{1,0:T(8,128)(2,1)S(1)}, bf16[128,256]{1,0:T(8,128)(2,1)S(1)}, u32[]{:S(2)}, u32[]{:S(2)}) collective-permute-start(bf16[128,256]{1,0:T(8,128)(2,1)S(1)} %fusion.27), channel_id=1, source_target_pairs={{12,0},{0,4},{4,8},{8,12},{13,1},{1,5},{5,9},{9,13},{14,2},{2,6},{... | collective-permute-start | bytes 196616 | tf_op jit(solution)/shard_map/ppermute | solution.py:18
  47.6 2.2 %collective-permute-done.5 = bf16[128,256]{1,0:T(8,128)(2,1)S(1)} collective-permute-done((bf16[128,256]{1,0:T(8,128)(2,1)S(1)}, bf16[128,256]{1,0:T(8,128)(2,1)S(1)}, u32[]{:S(2)}, u32[]{:S(2)}) %collective-permute-start.5) | collective-permute-done | bytes 65568 | tf_op jit(solution)/shard_map/ppermute | solution.py:18
  49.8 2.0 %collective-permute-done.4 = bf16[128,256]{1,0:T(8,128)(2,1)S(1)} collective-permute-done((bf16[128,256]{1,0:T(8,128)(2,1)S(1)}, bf16[128,256]{1,0:T(8,128)(2,1)S(1)}, u32[]{:S(2)}, u32[]{:S(2)}) %collective-permute-start.4) | collective-permute-done | bytes 65568 | tf_op jit(solution)/shard_map/ppermute | solution.py:18
  53.5 4.0 %fusion.19 = (f32[4,128]{0,1:T(8,128)S(1)}, f32[4,128,256]{2,0,1:T(4,128)S(1)}) fusion(f32[4,128]{0,1:T(8,128)S(1)} %copy-done.8, f32[32,128,256]{2,1,0:T(8,128)S(1)} %fusion.22, s32[32]{0:T(128)S(1)} %bitcast.158), kind=kOutput, calls=%fused_computation.39 | convolution fusion | flops 50724480 | bytes 4722816 | tf_op jit(solution)/shard_map/tr,tif->rif/dot_general | solution.py:59
  57.7 1.1 multiply_reduce_fusion
  61.1 3.8 %fusion.2 = bf16[3,128,256]{2,0,1:T(4,128)(2,1)S(1)} fusion(f32[32,128,256]{2,1,0:T(8,128)S(1)} %fusion.21, s32[32]{0:T(128)S(1)} %copy-done.11), kind=kOutput, calls=%fused_computation.6 | convolution fusion | flops 37748832 | bytes 4391040 | tf_op jit(solution)/shard_map/tc,tjf->cjf/dot_general | solution.py:52
  65.0 3.8 %collective-permute-start.7 = (bf16[128,256]{1,0:T(8,128)(2,1)S(1)}, bf16[128,256]{1,0:T(8,128)(2,1)S(1)}, u32[]{:S(2)}, u32[]{:S(2)}) collective-permute-start(bf16[128,256]{1,0:T(8,128)(2,1)S(1)} %get-tuple-element.12), channel_id=1, source_target_pairs={{4,0},{8,4},{12,8},{0,12},{5,1},{9,5},{13,9},{1,13},{6,2},{10,6},{... | collective-permute-start | bytes 196616 | tf_op jit(solution)/shard_map/ppermute | solution.py:18
  68.8 2.2 %collective-permute-done.6 = bf16[128,256]{1,0:T(8,128)(2,1)S(1)} collective-permute-done((bf16[128,256]{1,0:T(8,128)(2,1)S(1)}, bf16[128,256]{1,0:T(8,128)(2,1)S(1)}, u32[]{:S(2)}, u32[]{:S(2)}) %collective-permute-start.6) | collective-permute-done | bytes 65568 | tf_op jit(solution)/shard_map/ppermute | solution.py:18
  71.2 4.2 %collective-permute-start.9 = (bf16[128,256]{1,0:T(8,128)(2,1)S(1)}, bf16[128,256]{1,0:T(8,128)(2,1)S(1)}, u32[]{:S(2)}, u32[]{:S(2)}) collective-permute-start(bf16[128,256]{1,0:T(8,128)(2,1)S(1)} %fusion.30), channel_id=1, source_target_pairs={{4,0},{8,4},{12,8},{0,12},{5,1},{9,5},{13,9},{1,13},{6,2},{10,6},{... | collective-permute-start | bytes 196616 | tf_op jit(solution)/shard_map/ppermute | solution.py:18
  75.3 1.9 collective-permute-done.9
  77.2 4.2 %collective-permute-done.8 = bf16[128,256]{1,0:T(8,128)(2,1)S(1)} collective-permute-done((bf16[128,256]{1,0:T(8,128)(2,1)S(1)}, bf16[128,256]{1,0:T(8,128)(2,1)S(1)}, u32[]{:S(2)}, u32[]{:S(2)}) %collective-permute-start.8) | collective-permute-done | bytes 65568 | tf_op jit(solution)/shard_map/ppermute | solution.py:18
  82.9 3.8 %fusion = f32[4,128,256]{2,0,1:T(4,128)S(1)} fusion(f32[32,128,256]{2,1,0:T(8,128)S(1)} %fusion.20, s32[32]{0:T(128)S(1)} %bitcast.159), kind=kOutput, calls=%fused_computation.4 | convolution fusion | flops 50331776 | bytes 4718720 | tf_op jit(solution)/shard_map/tr,tif->rif/dot_general | solution.py:59
  87.9 0.8 copy.101
  89.5 2.3 %reduce.2 = bf16[256,512]{1,0:T(8,128)(2,1)S(1)} reduce(bf16[256,1,1,512]{3,2,1,0:T(2,128)(2,1)S(1)} %bitcast.138, bf16[]{:T(256)} %broadcast.232), dimensions={1,2}, to_apply=%bitcast.111.reduce_sub_computation | reduce | bytes 524290
  91.9 7.6 %all_to_all.33 = bf16[2,2,32768]{2,1,0:T(2,128)(2,1)S(1)} all-to-all(bf16[2,2,32768]{2,1,0:T(2,128)(2,1)S(1)} %reshape.235), channel_id=1, replica_groups=mesh['regroup'=2,'loop'=4,'replica'=4] {'regroup'}, dimensions={0} | all-to-all | bytes 524288 | tf_op jit(solution)/shard_map/all_to_all | solution.py:113
  99.8 0.8 copy.97
  100.7 46.7 %reduce-scatter.4.cloned.1.call-done = f32[32,256]{1,0:T(8,128)} async-done(((f32[256,256]{1,0:T(8,128)}), f32[32,256]{1,0:T(8,128)}) %reduce-scatter.4.cloned.1.call-update) | async-done | bytes 32784 | tf_op jit(solution)/shard_map/reduce_scatter | solution.py:117
  147.4 5.6 %all-gather = f32[128,256]{1,0:T(8,128)S(1)} all-gather(f32[32,256]{1,0:T(8,128)} %reduce-scatter.4.cloned.1.call-done), channel_id=2, replica_groups=mesh['regroup'=2,'loop'=4,'replica'=4] {'replica'}, dimensions={0}, use_global_device_ids=true | all-gather | bytes 163840 | tf_op jit(solution)/shard_map/all_gather | solution.py:11
  153.0 31.3 %all_gather.11 = f32[256,256]{1,0:T(8,128)S(1)} all-gather(f32[32,256]{1,0:T(8,128)S(1)} %reduce_sum.53), channel_id=1, replica_groups=mesh['regroup'=2,'loop'=4,'replica'=4] {'regroup','loop'}, dimensions={0}, use_global_device_ids=true | all-gather | bytes 294912 | tf_op jit(solution)/shard_map/all_gather | solution.py:121
  (95 shorter events, 16.5 us)
Async XLA Ops:
  7.2 22.9 %copy-start = (bf16[256,256]{1,0:T(8,128)(2,1)S(1)}, bf16[256,256]{1,0:T(8,128)(2,1)}, u32[]{:S(2)}) copy-start(bf16[256,256]{1,0:T(8,128)(2,1)} %param.8) | copy-start | bytes 393220
  7.2 17.3 %copy-start.18 = (s32[1,1,1,32]{3,2,1,0:T(1,128)S(1)}, s32[1,1,1,32]{3,2,1,0:T(1,128)}, u32[]{:S(2)}) copy-start(s32[1,1,1,32]{3,2,1,0:T(1,128)} %param.11) | copy-start | bytes 388
  7.2 17.8 %copy-start.14 = (s32[1,1,1,32]{3,2,1,0:T(1,128)S(1)}, s32[1,1,1,32]{3,2,1,0:T(1,128)}, u32[]{:S(2)}) copy-start(s32[1,1,1,32]{3,2,1,0:T(1,128)} %param.10) | copy-start | bytes 388
  8.6 16.4 %copy-start.9 = (s32[32]{0:T(128)}, s32[32]{0:T(128)S(1)}, u32[]{:S(2)}) copy-start(s32[32]{0:T(128)S(1)} %compare_select_fusion.8) | copy-start | bytes 388
  11.0 28.4 %collective-permute-start.2 = (bf16[128]{0:T(256)(128)(2,1)}, bf16[128]{0:T(256)(128)(2,1)}, u32[]{:S(2)}, u32[]{:S(2)}) collective-permute-start(bf16[128]{0:T(256)(128)(2,1)} %get-tuple-element.13), channel_id=1, source_target_pairs={{12,0},{0,4},{4,8},{8,12},{13,1},{1,5},{5,9},{9,13},{14,2},{2,6},{... | collective-permute-start | bytes 776 | tf_op jit(solution)/shard_map/ppermute | solution.py:18
  14.0 25.4 %collective-permute-start.3 = (bf16[128]{0:T(256)(128)(2,1)}, bf16[128]{0:T(256)(128)(2,1)}, u32[]{:S(2)}, u32[]{:S(2)}) collective-permute-start(bf16[128]{0:T(256)(128)(2,1)} %get-tuple-element.14), channel_id=1, source_target_pairs={{4,0},{8,4},{12,8},{0,12},{5,1},{9,5},{13,9},{1,13},{6,2},{10,6},{... | collective-permute-start | bytes 776 | tf_op jit(solution)/shard_map/ppermute | solution.py:18
  20.9 8.6 %all-to-all-start = ((bf16[2,2,32768]{2,1,0:T(2,128)(2,1)}), bf16[2,2,32768]{2,1,0:T(2,128)(2,1)S(1)}, u32[]{:S(2)}, u32[]{:S(2)}) async-start(bf16[2,2,32768]{2,1,0:T(2,128)(2,1)} %reshape.233), calls=%async_computation | async-start | bytes 524288 | tf_op jit(solution)/shard_map/all_to_all | solution.py:26
  24.4 123.0 %reduce-scatter.4.cloned.1.call-start = ((), (), s32[]{:S(2)}) async-start(), calls=%async_computation.3 | async-start | bytes 294912 | tf_op jit(solution)/shard_map/reduce_scatter | solution.py:117
  30.0 1.1 copy-start.4
  31.1 1.2 copy-start.1
  32.3 0.8 copy-start.10
  33.1 14.5 %copy-start.17 = (s32[32]{0:T(128)S(1)}, s32[32]{0:T(128)}, u32[]{:S(2)}) copy-start(s32[32]{0:T(128)} %fusion.43) | copy-start | bytes 388
  37.3 4.3 %collective-permute-start.1 = (bf16[128,256]{1,0:T(8,128)(2,1)S(1)}, bf16[128,256]{1,0:T(8,128)(2,1)S(1)}, u32[]{:S(2)}, u32[]{:S(2)}) collective-permute-start(bf16[128,256]{1,0:T(8,128)(2,1)S(1)} %bitcast.148), channel_id=1, source_target_pairs={{4,0},{8,4},{12,8},{0,12},{5,1},{9,5},{13,9},{1,13},{6,2},{10,6},{... | collective-permute-start | bytes 196616 | tf_op jit(solution)/shard_map/ppermute | solution.py:18
  39.4 6.1 %collective-permute-start = (bf16[128,256]{1,0:T(8,128)(2,1)S(1)}, bf16[128,256]{1,0:T(8,128)(2,1)S(1)}, u32[]{:S(2)}, u32[]{:S(2)}) collective-permute-start(bf16[128,256]{1,0:T(8,128)(2,1)S(1)} %bitcast.147), channel_id=1, source_target_pairs={{12,0},{0,4},{4,8},{8,12},{13,1},{1,5},{5,9},{9,13},{14,2},{2,6},{... | collective-permute-start | bytes 196616 | tf_op jit(solution)/shard_map/ppermute | solution.py:18
  40.0 11.9 %copy-start.12 = (f32[128]{0:T(128)}, f32[128]{0:T(128)S(1)}, u32[]{:S(2)}) copy-start(f32[128]{0:T(128)S(1)} %fusion.48) | copy-start | bytes 1540
  45.5 4.3 %collective-permute-start.5 = (bf16[128,256]{1,0:T(8,128)(2,1)S(1)}, bf16[128,256]{1,0:T(8,128)(2,1)S(1)}, u32[]{:S(2)}, u32[]{:S(2)}) collective-permute-start(bf16[128,256]{1,0:T(8,128)(2,1)S(1)} %fusion.27), channel_id=1, source_target_pairs={{4,0},{8,4},{12,8},{0,12},{5,1},{9,5},{13,9},{1,13},{6,2},{10,6},{... | collective-permute-start | bytes 196616 | tf_op jit(solution)/shard_map/ppermute | solution.py:18
  45.6 6.3 %collective-permute-start.4 = (bf16[128,256]{1,0:T(8,128)(2,1)S(1)}, bf16[128,256]{1,0:T(8,128)(2,1)S(1)}, u32[]{:S(2)}, u32[]{:S(2)}) collective-permute-start(bf16[128,256]{1,0:T(8,128)(2,1)S(1)} %fusion.27), channel_id=1, source_target_pairs={{12,0},{0,4},{4,8},{8,12},{13,1},{1,5},{5,9},{9,13},{14,2},{2,6},{... | collective-permute-start | bytes 196616 | tf_op jit(solution)/shard_map/ppermute | solution.py:18
  52.6 0.8 copy-start.8
  52.6 0.8 copy-start.15
  53.5 4.2 %copy-start.6 = (f32[512,256]{1,0:T(8,128)S(1)}, f32[512,256]{1,0:T(8,128)}, u32[]{:S(2)}) copy-start(f32[512,256]{1,0:T(8,128)} %get-tuple-element.16) | copy-start | bytes 1572868
  53.5 4.2 %copy-start.7 = (bf16[1,1,1,512,256]{4,3,2,1,0:T(8,128)(2,1)S(1)}, bf16[1,1,1,512,256]{4,3,2,1,0:T(8,128)(2,1)}, u32[]{:S(2)}) copy-start(bf16[1,1,1,512,256]{4,3,2,1,0:T(8,128)(2,1)} %param.13) | copy-start | bytes 786436
  58.8 0.8 copy-start.2
  60.3 0.8 copy-start.11
  61.1 10.0 %copy-start.13 = (f32[128]{0:T(128)S(1)}, f32[128]{0:T(128)}, u32[]{:S(2)}) copy-start(f32[128]{0:T(128)} %copy-done.12) | copy-start | bytes 1540
  65.0 6.1 %collective-permute-start.6 = (bf16[128,256]{1,0:T(8,128)(2,1)S(1)}, bf16[128,256]{1,0:T(8,128)(2,1)S(1)}, u32[]{:S(2)}, u32[]{:S(2)}) collective-permute-start(bf16[128,256]{1,0:T(8,128)(2,1)S(1)} %get-tuple-element.11), channel_id=1, source_target_pairs={{12,0},{0,4},{4,8},{8,12},{13,1},{1,5},{5,9},{9,13},{14,2},{2,6},{... | collective-permute-start | bytes 196616 | tf_op jit(solution)/shard_map/ppermute | solution.py:18
  65.0 6.1 %collective-permute-start.7 = (bf16[128,256]{1,0:T(8,128)(2,1)S(1)}, bf16[128,256]{1,0:T(8,128)(2,1)S(1)}, u32[]{:S(2)}, u32[]{:S(2)}) collective-permute-start(bf16[128,256]{1,0:T(8,128)(2,1)S(1)} %get-tuple-element.12), channel_id=1, source_target_pairs={{4,0},{8,4},{12,8},{0,12},{5,1},{9,5},{13,9},{1,13},{6,2},{10,6},{... | collective-permute-start | bytes 196616 | tf_op jit(solution)/shard_map/ppermute | solution.py:18
  71.2 6.1 %collective-permute-start.9 = (bf16[128,256]{1,0:T(8,128)(2,1)S(1)}, bf16[128,256]{1,0:T(8,128)(2,1)S(1)}, u32[]{:S(2)}, u32[]{:S(2)}) collective-permute-start(bf16[128,256]{1,0:T(8,128)(2,1)S(1)} %fusion.30), channel_id=1, source_target_pairs={{4,0},{8,4},{12,8},{0,12},{5,1},{9,5},{13,9},{1,13},{6,2},{10,6},{... | collective-permute-start | bytes 196616 | tf_op jit(solution)/shard_map/ppermute | solution.py:18
  75.3 6.1 %collective-permute-start.8 = (bf16[128,256]{1,0:T(8,128)(2,1)S(1)}, bf16[128,256]{1,0:T(8,128)(2,1)S(1)}, u32[]{:S(2)}, u32[]{:S(2)}) collective-permute-start(bf16[128,256]{1,0:T(8,128)(2,1)S(1)} %fusion.30), channel_id=1, source_target_pairs={{12,0},{0,4},{4,8},{8,12},{13,1},{1,5},{5,9},{9,13},{14,2},{2,6},{... | collective-permute-start | bytes 196616 | tf_op jit(solution)/shard_map/ppermute | solution.py:18
  82.1 0.7 copy-start.16
  82.8 3.9 %copy-start.3 = (f32[512,256]{1,0:T(8,128)S(1)}, f32[512,256]{1,0:T(8,128)}, u32[]{:S(2)}) copy-start(f32[512,256]{1,0:T(8,128)} %copy-done.2) | copy-start | bytes 1572868
  86.7 1.0 copy-start.5
Sparse Core Ops, SparseCore 0:
  88.9 58.4 reduce-scatter.3
